TPU v7x, 32 devices: a whole 2x2x4 slice. The times are simulated.
32 devices in a mesh: dp: 4 (over y, core), bucket: 8 (over z, x).
Axes of the slice: x: 2, y: 2, z: 4, core: 2. Of those that a mesh axis runs over, the one named last changes fastest.
Arguments:
- frames: bfloat16 [49152, 512], P(('dp', 'bucket')), may hold values from -60 to 60, as said below
- lengths: int32 [4, 256], P('dp'), may hold values from 1 to 48, as said below
- owners: int32 [4, 256], P('dp'), may hold values from 0 to 7, as said below
- upstream: bfloat16 [24576, 512], P(('dp', 'bucket')), may hold values from -6 to 6
- ln_gain: float32 [512], replicated, may hold values from 0.1 to 1.9
- w_in: bfloat16 [512, 1024], replicated, may hold values from -0.25 to 0.25
- w_dw: float32 [512, 31], replicated, may hold values from -1 to 1
- bn_gain: float32 [512], replicated, may hold values from 0.1 to 1.9
- bn_bias: float32 [512], replicated, may hold values from -3 to 3
- w_out: bfloat16 [512, 512], replicated, may hold values from -0.25 to 0.25
Outputs:
- out_frames: bfloat16 [24576, 512], P(('dp', 'bucket'))
- grad_frames: bfloat16 [49152, 512], P(('dp', 'bucket'))
- grad_w_in: float32 [512, 1024], P('bucket')
- grad_w_out: float32 [512, 512], P('bucket')
- grad_w_dw: float32 [512, 31], P('bucket')
- grad_ln_gain: float32 [512], P('bucket')
- grad_bn_gain: float32 [512], replicated
- grad_bn_bias: float32 [512], replicated
Inputs may be any that keep to these rules, and one draw needn't show every extreme that they name: `frames`: frame rows past an utterance's length are not read. In each group every owner receives exactly 4 utterances from each loader shard, their lengths sum to exactly 768 with one of exactly 48, and the lengths an owner receives do not fall with the loader index. `owners`: in each group and loader shard every owner index appears exactly 4 times.
All inputs are finite; a program needn't handle non-finite values.
Results may differ from a plain program's by a relative error of at most 0.013.
Values may be sent and summed in bfloat16 or wider, within the bound.
A program may use at most 128 MiB of HBM per device.

v0:
```python
import jax
import jax.numpy as jnp
from jax import lax
from jax.sharding import PartitionSpec as P

EPSILON = 1e-05


def normalize_rows(frame_rows, ln_gain):
    values = frame_rows.astype(jnp.float32)
    centred = values - jnp.mean(values, axis=1, keepdims=True)
    inverse = lax.rsqrt(jnp.mean(centred * centred, axis=1, keepdims=True) + EPSILON)
    normed = centred * inverse
    return ((normed * ln_gain).astype(jnp.bfloat16), normed, inverse)


def normalize_back(grad_h, normed, inverse, ln_gain):
    scaled = grad_h * ln_gain
    inner_sum = jnp.mean(scaled * normed, axis=1, keepdims=True)
    return inverse * (scaled - jnp.mean(scaled, axis=1, keepdims=True) - normed * inner_sum)


def conv_forward(gated_rows, segment, w_dw):
    width_half = w_dw.shape[1] // 2
    length_all = gated_rows.shape[1]
    padded = jnp.pad(gated_rows, ((0, 0), (width_half, width_half), (0, 0)))
    seg_pad = jnp.pad(segment, ((0, 0), (width_half, width_half)), constant_values=-1)
    result = jnp.zeros(gated_rows.shape, jnp.float32)
    for offset in range(w_dw.shape[1]):
        same_seg = (seg_pad[:, offset : offset + length_all] == segment)[:, :, None]
        shifted = padded[:, offset : offset + length_all].astype(jnp.float32)
        result = result + jnp.where(same_seg, shifted, 0.0) * w_dw[:, offset]
    return result


def conv_backward(grad_conv, gated_rows, segment, w_dw):
    width_half = w_dw.shape[1] // 2
    length_all = gated_rows.shape[1]
    padded = jnp.pad(gated_rows, ((0, 0), (width_half, width_half), (0, 0)))
    grad_pad = jnp.pad(grad_conv, ((0, 0), (width_half, width_half), (0, 0)))
    seg_pad = jnp.pad(segment, ((0, 0), (width_half, width_half)), constant_values=-1)
    grad_gated = jnp.zeros(grad_conv.shape, jnp.float32)
    grad_cols = []
    for offset in range(w_dw.shape[1]):
        same_fwd = (seg_pad[:, offset : offset + length_all] == segment)[:, :, None]
        shifted = jnp.where(
            same_fwd, padded[:, offset : offset + length_all].astype(jnp.float32), 0.0
        )
        grad_cols.append(jnp.sum(shifted * grad_conv, axis=(0, 1)))
        back_start = 2 * width_half - offset
        same_back = (seg_pad[:, back_start : back_start + length_all] == segment)[:, :, None]
        grad_gated = (
            grad_gated
            + jnp.where(same_back, grad_pad[:, back_start : back_start + length_all], 0.0)
            * w_dw[:, offset]
        )
    return (grad_gated, jnp.stack(grad_cols, axis=1))


def local(frames, lengths, owners, upstream, ln_gain, w_in, w_dw, bn_gain, bn_bias, w_out):
    loaders = lax.axis_size("bucket")
    own_index = lax.axis_index("bucket")
    feature_count = frames.shape[1]
    slot_count = lengths.shape[1] // loaders
    span_max = frames.shape[0] // slot_count
    pair_count = slot_count // loaders
    own_rows = upstream.shape[0]
    total_frames = float(own_rows * loaders * lax.axis_size("dp"))
    lens_all = lengths[0].reshape(loaders, slot_count)
    dest_all = owners[0].reshape(loaders, slot_count)
    owner_ids = jnp.arange(loaders, dtype=jnp.int32)
    onehot = (dest_all[:, :, None] == owner_ids[None, None, :]).astype(jnp.int32)
    earlier = jnp.cumsum(onehot, axis=1) - onehot
    ranking = jnp.sum(earlier * onehot, axis=2)
    send_pos = dest_all * pair_count + ranking
    my_pos = lax.dynamic_index_in_dim(send_pos, own_index, 0, keepdims=False)
    send_order = (
        jnp.zeros((slot_count,), jnp.int32).at[my_pos].set(jnp.arange(slot_count, dtype=jnp.int32))
    )
    slot_frames = frames.reshape(slot_count, span_max, feature_count)
    outgoing = jnp.take(slot_frames, send_order, axis=0).reshape(
        loaders, pair_count, span_max, feature_count
    )
    incoming = lax.all_to_all(outgoing, "bucket", split_axis=0, concat_axis=0, tiled=True)
    incoming_rows = incoming.reshape(slot_count * span_max, feature_count)
    pair_ids = jnp.arange(pair_count, dtype=jnp.int32)
    to_me = (dest_all == own_index)[:, :, None] & (ranking[:, :, None] == pair_ids[None, None, :])
    recv_lens = jnp.sum(jnp.where(to_me, lens_all[:, :, None], 0), axis=1).reshape(-1)
    starts = jnp.cumsum(recv_lens) - recv_lens
    position = jnp.arange(span_max, dtype=jnp.int32)
    slot_valid = position[None, :] < recv_lens[:, None]
    row_ids = jnp.arange(own_rows, dtype=jnp.int32)
    row_slot = jnp.sum((starts[None, :] <= row_ids[:, None]).astype(jnp.int32), axis=1) - 1
    row_offset = row_ids - jnp.take(starts, row_slot)
    packed_source = row_slot * span_max + row_offset
    slot_target = jnp.minimum(
        jnp.where(slot_valid, starts[:, None] + position[None, :], own_rows - 1), own_rows - 1
    ).reshape(-1)
    slot_valid_flat = slot_valid.reshape(-1)
    segment = jnp.broadcast_to(
        jnp.arange(slot_count, dtype=jnp.int32)[:, None], (slot_count, span_max)
    )
    work_grad = jnp.where(slot_valid_flat[:, None], jnp.take(upstream, slot_target, axis=0), 0)
    group_count = segment.shape[0]
    group_length = segment.shape[1]
    normed_h, normed, inverse = normalize_rows(incoming_rows, ln_gain)
    projected = jnp.dot(normed_h, w_in, preferred_element_type=jnp.float32)
    linear = projected[:, :feature_count]
    gate_sig = jax.nn.sigmoid(projected[:, feature_count:])
    gated_rows = jnp.where(slot_valid_flat[:, None], linear * gate_sig, 0.0).astype(jnp.bfloat16)
    gated_blocks = gated_rows.reshape(group_count, group_length, feature_count)
    conv_rows = conv_forward(gated_blocks, segment, w_dw).reshape(-1, feature_count)
    masked = jnp.where(slot_valid_flat[:, None], conv_rows, 0.0)
    first_sum, second_sum = lax.psum(
        (jnp.sum(masked, axis=0), jnp.sum(masked * masked, axis=0)), ("dp", "bucket")
    )
    centre = first_sum / total_frames
    variance = second_sum / total_frames - centre * centre
    bn_inverse = lax.rsqrt(variance + EPSILON)
    bn_normed = (conv_rows - centre) * bn_inverse
    bn_value = bn_normed * bn_gain + bn_bias
    bn_sig = jax.nn.sigmoid(bn_value)
    swished = (bn_value * bn_sig).astype(jnp.bfloat16)
    out_rows = jnp.dot(swished, w_out, preferred_element_type=jnp.float32).astype(jnp.bfloat16)
    out_frames = jnp.take(out_rows, packed_source, axis=0)
    grad_wout = jnp.einsum("rd,re->de", swished, work_grad, preferred_element_type=jnp.float32)
    grad_swish = jnp.einsum("re,de->rd", work_grad, w_out, preferred_element_type=jnp.float32)
    grad_bn_rows = grad_swish * (bn_sig * (1.0 + bn_value * (1.0 - bn_sig)))
    bias_total, gain_total = lax.psum(
        (jnp.sum(grad_bn_rows, axis=0), jnp.sum(grad_bn_rows * bn_normed, axis=0)), ("dp", "bucket")
    )
    grad_conv = jnp.where(
        slot_valid_flat[:, None],
        bn_gain
        * bn_inverse
        * (grad_bn_rows - bias_total / total_frames - bn_normed * (gain_total / total_frames)),
        0.0,
    )
    grad_gated, grad_wdw = conv_backward(
        grad_conv.reshape(group_count, group_length, feature_count), gated_blocks, segment, w_dw
    )
    grad_gated = jnp.where(slot_valid_flat[:, None], grad_gated.reshape(-1, feature_count), 0.0)
    grad_proj = jnp.concatenate(
        [grad_gated * gate_sig, grad_gated * linear * gate_sig * (1.0 - gate_sig)], axis=1
    ).astype(jnp.bfloat16)
    grad_win = jnp.einsum("rd,rf->df", normed_h, grad_proj, preferred_element_type=jnp.float32)
    grad_h = jnp.einsum("rf,df->rd", grad_proj, w_in, preferred_element_type=jnp.float32)
    grad_ln = jnp.sum(grad_h * normed, axis=0)
    grad_work = jnp.where(
        slot_valid_flat[:, None], normalize_back(grad_h, normed, inverse, ln_gain), 0.0
    ).astype(jnp.bfloat16)
    returned = lax.all_to_all(
        grad_work.reshape(loaders, pair_count, span_max, feature_count),
        "bucket",
        split_axis=0,
        concat_axis=0,
        tiled=True,
    )
    grad_frames = jnp.take(
        returned.reshape(slot_count, span_max, feature_count), my_pos, axis=0
    ).reshape(-1, feature_count)
    row_sums = (
        lax.psum_scatter(grad_win, "bucket", scatter_dimension=0, tiled=True),
        lax.psum_scatter(grad_wout, "bucket", scatter_dimension=0, tiled=True),
        lax.psum_scatter(grad_wdw, "bucket", scatter_dimension=0, tiled=True),
        lax.psum_scatter(grad_ln, "bucket", scatter_dimension=0, tiled=True),
    )
    shares = (
        lax.psum(row_sums[0].astype(jnp.bfloat16), "dp").astype(jnp.float32),
        lax.psum(row_sums[1].astype(jnp.bfloat16), "dp").astype(jnp.float32),
        lax.psum(row_sums[2].astype(jnp.bfloat16), "dp").astype(jnp.float32),
        lax.psum(row_sums[3].astype(jnp.bfloat16), "dp").astype(jnp.float32),
    )
    return (
        out_frames,
        grad_frames,
        shares[0],
        shares[1],
        shares[2],
        shares[3],
        gain_total,
        bias_total,
    )


def solution(mesh):
    placed = (
        P(("dp", "bucket"), None),
        P("dp", None),
        P("dp", None),
        P(("dp", "bucket"), None),
        P(),
        P(),
        P(),
        P(),
        P(),
        P(),
    )
    return jax.shard_map(
        local,
        mesh=mesh,
        in_specs=placed,
        out_specs=(
            P(("dp", "bucket"), None),
            P(("dp", "bucket"), None),
            P("bucket", None),
            P("bucket", None),
            P("bucket", None),
            P("bucket"),
            P(),
            P(),
        ),
        check_vma=False,
    )
```

profile of v0, /device:TPU:0, one launch (start us, length us, event | category | flops | bytes accessed | tf_op | source)
XLA Modules:
  0.0 468.8 jit_solution(478238532868027686)
XLA Ops:
  7.7 1.3 reduce.68
  10.8 1.8 gather_fusion.2
  12.6 2.8 broadcast_select_fusion.1
  15.4 7.3 %all-to-all-start = ((bf16[8,4,48,512]{3,2,1,0:T(8,128)(2,1)}), bf16[8,4,48,512]{3,2,1,0:T(8,128)(2,1)}, u32[]{:S(2)}, u32[]{:S(2)}) async-start(bf16[8,4,48,512]{3,2,1,0:T(8,128)(2,1)} %bitcast.243), calls=%async_computation | async-start | bytes 3145728 | tf_op jit(solution)/shard_map/all_to_all | solution.py:84
  24.5 5.4 %gather_fusion.1 = bf16[1536,512]{1,0:T(8,128)(2,1)} fusion(bf16[768,512]{1,0:T(8,128)(2,1)S(1)} %copy-done.1, s32[2048]{0:T(1024)S(1)} %pad_clamp_fusion), kind=kCustom, calls=%fused_computation.3 | custom fusion | bytes 3151872 | tf_op jit(solution)/shard_map/jit(_take)/gather | solution.py:103
  30.1 29.7 %all-to-all-done = bf16[8,4,48,512]{3,2,1,0:T(8,128)(2,1)} async-done(((bf16[8,4,48,512]{3,2,1,0:T(8,128)(2,1)}), bf16[8,4,48,512]{3,2,1,0:T(8,128)(2,1)}, u32[]{:S(2)}, u32[]{:S(2)}) %all-to-all-start) | async-done | bytes 1572896 | tf_op jit(solution)/shard_map/all_to_all | solution.py:84
  59.8 1.7 convert_reduce_fusion
  61.6 2.1 multiply_reduce_fusion.35
  63.8 2.0 multiply_convert_fusion.3
  65.8 1.8 fusion.119
  68.0 1.4 select_convert_fusion.1
  69.4 0.9 copy-done.3
  70.6 20.7 %select_reduce_fusion = (f32[512]{0:T(512)S(1)}, f32[512]{0:T(512)S(1)}, f32[32,48,512]{2,1,0:T(8,128)}) fusion(pred[32,48]{1,0:T(8,128)(4,1)S(1)} %iota_compare_fusion.3, f32[512]{0:T(512)S(1)} %bitcast.355, pred[32,48]{1,0:T(8,128)(4,1)S(1)} %bitcast.323, f32[512]{0:T(512)S(1)} %bitcast.357, pred[32,48]{1,0:T(8,128)(4,1)S(1)} %bitcast.320, ...), kind=kLoop, calls=%fused_computation.243 | loop fusion | flops 99089408 | bytes 4833792 | tf_op jit(solution)/shard_map/reduce_sum | solution.py:115
  91.3 37.9 %all-reduce.4 = (f32[512]{0:T(512)S(1)}, f32[512]{0:T(512)S(1)}) all-reduce(f32[512]{0:T(512)S(1)} %get-tuple-element.42, f32[512]{0:T(512)S(1)} %get-tuple-element.41), channel_id=1, replica_groups=mesh['dp'=4,'bucket'=8] {'dp','bucket'}, use_global_device_ids=true, to_apply=%region_11.13 | all-reduce | flops 1024 | bytes 8192 | tf_op jit(solution)/shard_map/psum | solution.py:114
  129.2 4.2 multiply_convert_fusion.2
  133.4 4.3 fusion.111
  137.7 41.4 %all-reduce.3 = (f32[512]{0:T(512)S(1)}, f32[512]{0:T(512)S(1)}) all-reduce(f32[512]{0:T(512)S(1)} %get-tuple-element.45, f32[512]{0:T(512)S(1)} %get-tuple-element.44), channel_id=1, replica_groups=mesh['dp'=4,'bucket'=8] {'dp','bucket'}, use_global_device_ids=true, to_apply=%region_15.17 | all-reduce | flops 1024 | bytes 8192 | tf_op jit(solution)/shard_map/psum | solution.py:129
  179.6 5.5 %multiply_reduce_fusion.16 = (f32[512]{0:T(512)S(1)}, f32[1536,512]{1,0:T(8,128)S(1)}) fusion(f32[1536,512]{1,0:T(8,128)} %copy-done.4, f32[512]{0:T(512)S(1)} %get-tuple-element.164, f32[1536,512]{1,0:T(8,128)} %get-tuple-element.162, f32[512]{0:T(512)S(1)} %get-tuple-element.165, f32[512]{0:T(512)S(1)} %get-tuple-element.83, pred[1536]{0:T(1024)(128)(4,1)S(1)} %lt.126, ...), kind=kLoop, calls=%fused_computation.182 | loop fusion | flops 11009536 | bytes 15738368 | tf_op jit(solution)/shard_map/reduce_sum | solution.py:49
  185.2 1.9 multiply_reduce_fusion.29
  187.1 7.1 %multiply_reduce_fusion.10 = (f32[512]{0:T(512)S(1)}, f32[512]{0:T(512)S(1)}, f32[512]{0:T(512)S(1)}, f32[512]{0:T(512)S(1)}, f32[512]{0:T(512)S(1)}, /*index=5*...) fusion(f32[32,48,512]{2,1,0:T(8,128)S(1)} %bitcast.234, pred[32,48]{1,0:T(8,128)(4,1)S(1)} %bitcast.297, ...), kind=kLoop, calls=%fused_computation.176 | loop fusion | flops 28306944 | bytes 4750848 | tf_op jit(solution)/shard_map/reduce_sum | solution.py:49
  194.2 6.7 %multiply_reduce_fusion.20 = (f32[512]{0:T(512)S(1)}, f32[512]{0:T(512)S(1)}, f32[512]{0:T(512)S(1)}, f32[512]{0:T(512)S(1)}, f32[512]{0:T(512)S(1)}, /*index=5*...) fusion(f32[32,48,512]{2,1,0:T(8,128)S(1)} %bitcast.235, pred[32,48]{1,0:T(8,128)(4,1)S(1)} %bitcast.270, ...), kind=kLoop, calls=%fused_computation.186 | loop fusion | flops 28306944 | bytes 4750848 | tf_op jit(solution)/shard_map/reduce_sum | solution.py:49
  200.9 6.5 %multiply_reduce_fusion.1 = (f32[512]{0:T(512)S(1)}, f32[512]{0:T(512)S(1)}, f32[512]{0:T(512)S(1)}, f32[512]{0:T(512)S(1)}, f32[512]{0:T(512)S(1)}, /*index=5*/...) fusion(f32[32,48,512]{2,1,0:T(8,128)S(1)} %bitcast.236, pred[32,48]{1,0:T(8,128)(4,1)S(1)} %bitcast.324, ...), kind=kLoop, calls=%fused_computation.167 | loop fusion | flops 28306944 | bytes 4750848 | tf_op jit(solution)/shard_map/reduce_sum | solution.py:49
  207.5 0.8 copy.41
  208.5 4.0 fusion.110
  212.8 49.1 %fusion.73 = f32[32,48,512]{2,1,0:T(8,128)} fusion(f32[32,48,512]{2,1,0:T(8,128)} %bitcast.237, f32[512]{0:T(512)S(1)} %bitcast.356, f32[512]{0:T(512)S(1)} %bitcast.358, f32[512]{0:T(512)S(1)} %bitcast.362, f32[512]{0:T(512)S(1)} %bitcast.364, f32[512]{0:T(512)S(1)} %bitcast.366, f32[512]{0:T(512)S(1)} %bitcast.368, f32[512]{0:T(512)S(1)} %bitcast.370, ...), kind=kLoop, calls=%fused_computation.139 | loop fusion | flops 71565312 | bytes 6401024 | tf_op jit(solution)/shard_map/add | solution.py:53
  261.9 4.7 %multiply_convert_fusion.1 = (bf16[1536,512]{1,0:T(8,128)(2,1)S(1)}, bf16[1536,512]{1,0:T(8,128)(2,1)S(1)}) fusion(f32[32,48,512]{2,1,0:T(8,128)} %fusion.73, pred[1536]{0:T(1024)(128)(4,1)S(1)} %lt.126, f32[1536,1024]{1,0:T(8,128)} %copy-done.3), kind=kLoop, calls=%fused_computation.201 | loop fusion | flops 8650752 | bytes 12584448 | tf_op jit(solution)/shard_map/convert.1
  266.6 1.1 copy-done.8
  267.7 3.2 fusion.95
  270.9 4.8 %multiply_reduce_fusion = (f32[512]{0:T(512)S(1)}, f32[1536]{0:T(1024)S(1)}, f32[1536]{0:T(1024)S(1)}, f32[1536,512]{1,0:T(8,128)S(1)}) fusion(bf16[8,4,48,512]{3,2,1,0:T(8,128)(2,1)} %all-to-all-done, f32[1536]{0:T(1024)S(1)} %rsqrt.15, f32[1536]{0:T(1024)S(1)} %div.33, f32[512]{0:T(512)S(1)} %copy-done.41, bf16[512,1024]{1,0:T(8,128)(2,1)} %param.17, ...), kind=kOutput, calls=%fused_computation.166 | convolution fusion | flops 1623978496 | bytes 8941568 | tf_op jit(solution)/shard_map/rf,df->rd/dot_general | solution.py:147
  275.8 3.4 select_convert_fusion
  279.2 5.2 %all-to-all-start.1 = ((bf16[8,4,48,512]{3,2,1,0:T(8,128)(2,1)}), bf16[8,4,48,512]{3,2,1,0:T(8,128)(2,1)}, u32[]{:S(2)}, u32[]{:S(2)}) async-start(bf16[8,4,48,512]{3,2,1,0:T(8,128)(2,1)} %bitcast.73), calls=%async_computation.1 | async-start | bytes 3145728 | tf_op jit(solution)/shard_map/all_to_all | solution.py:152
  286.5 4.5 fusion.102
  292.0 16.2 %compare_and_fusion.1 = (pred[768]{0:T(1024)(128)(4,1)S(1)}, s32[768]{0:T(1024)S(1)}) fusion(s32[768]{0:T(1024)S(1)} %convert_reduce_fusion.1, pred[768]{0:T(1024)(128)(4,1)S(1)} %get-tuple-element.70, pred[768]{0:T(1024)(128)(4,1)S(1)} %get-tuple-element.68, pred[768]{0:T(1024)(128)(4,1)S(1)} %get-tuple-element.69, ...), kind=kLoop, calls=%fused_computation.315 | loop fusion | flops 32256 | bytes 29284 | tf_op jit(solution)/shard_map/jit(_take)/and | solution.py:125
  308.3 2.5 convolution_convert_fusion
  310.8 3.3 gather_fusion
  314.1 21.9 %all-reduce.2 = bf16[512]{0:T(512)(128)(2,1)S(1)} all-reduce(f32[512]{0:T(512)S(1)} %get-tuple-element.9), channel_id=5, replica_groups=mesh['dp'=4,'bucket'=8] {'bucket'}, use_global_device_ids=true, to_apply=%region_56.58.clone | all-reduce | flops 512 | bytes 3072
  336.1 2.2 broadcast_select_fusion.2
  338.3 0.8 copy.42
  339.1 5.9 %all-reduce.5 = (bf16[64,31]{0,1:T(8,128)(2,1)S(1)}, bf16[64]{0:T(256)(128)(2,1)S(1)}) all-reduce(bf16[64,31]{0,1:T(8,128)(2,1)S(1)} %copy.42, bf16[64]{0:T(256)(128)(2,1)S(1)} %dynamic-slice.3), channel_id=1, replica_groups=mesh['dp'=4,'bucket'=8] {'dp'}, use_global_device_ids=true, to_apply=%region_54.56 | all-reduce | flops 2048 | bytes 8192 | tf_op jit(solution)/shard_map/psum | solution.py:171
  346.2 7.7 %reduce-scatter.8.cloned.1.call-done = f32[64,512]{1,0:T(8,128)} async-done(((f32[512,512]{1,0:T(8,128)}), f32[64,512]{1,0:T(8,128)}) %reduce-scatter.8.cloned.1.call-update) | async-done | bytes 131088 | tf_op jit(solution)/shard_map/reduce_scatter | solution.py:164
  353.8 1.5 convert_element_type.233
  355.4 2.1 gather_fusion.3
  357.5 67.6 %reduce-scatter.6.cloned.1.call-done = f32[64,1024]{1,0:T(8,128)} async-done(((f32[512,1024]{1,0:T(8,128)}), f32[64,1024]{1,0:T(8,128)}) %reduce-scatter.6.cloned.1.call-update) | async-done | bytes 262160 | tf_op jit(solution)/shard_map/reduce_scatter | solution.py:163
  425.0 1.6 convert_element_type.231
  426.7 1.4 broadcast_select_fusion
  428.0 31.1 %all-reduce.9.cloned.1.call-done = (bf16[64,1024]{1,0:T(8,128)(2,1)}, bf16[64,512]{1,0:T(8,128)(2,1)}) async-done(((bf16[64,1024]{1,0:T(8,128)(2,1)}, bf16[64,512]{1,0:T(8,128)(2,1)}), (bf16[64,1024]{1,0:T(8,128)(2,1)}, bf16[64,512]{1,0:T(8,128)(2,1)})) %all-reduce.9.cloned.1.call-update) | async-done | bytes 196624 | tf_op jit(solution)/shard_map/psum | solution.py:169
  459.1 1.6 convert_element_type.232
  460.7 1.5 convert_element_type.234
  (162 shorter events, 9.2 us)
Async XLA Ops:
  7.2 3.6 copy-start
  12.6 10.2 %copy-start.46 = (s32[1,256]{1,0:T(1,128)S(1)}, s32[1,256]{1,0:T(1,128)}, u32[]{:S(2)}) copy-start(s32[1,256]{1,0:T(1,128)} %param.13) | copy-start | bytes 3076
  12.6 12.0 %copy-start.1 = (bf16[768,512]{1,0:T(8,128)(2,1)S(1)}, bf16[768,512]{1,0:T(8,128)(2,1)}, u32[]{:S(2)}) copy-start(bf16[768,512]{1,0:T(8,128)(2,1)} %param.15) | copy-start | bytes 2359300
  15.4 44.4 %all-to-all-start = ((bf16[8,4,48,512]{3,2,1,0:T(8,128)(2,1)}), bf16[8,4,48,512]{3,2,1,0:T(8,128)(2,1)}, u32[]{:S(2)}, u32[]{:S(2)}) async-start(bf16[8,4,48,512]{3,2,1,0:T(8,128)(2,1)} %bitcast.243), calls=%async_computation | async-start | bytes 3145728 | tf_op jit(solution)/shard_map/all_to_all | solution.py:84
  22.7 315.6 %reduce-scatter.10.cloned.1.call-start = ((), (), s32[]{:S(2)}) async-start(), calls=%async_computation.7 | async-start | bytes 294912
  24.5 5.4 %copy-start.9 = (f32[512,31]{0,1:T(8,128)S(1)}, f32[512,31]{0,1:T(8,128)}, u32[]{:S(2)}) copy-start(f32[512,31]{0,1:T(8,128)} %param.18) | copy-start | bytes 190468
  29.9 33.8 %copy-start.41 = (f32[512]{0:T(512)S(1)}, f32[512]{0:T(512)}, u32[]{:S(2)}) copy-start(f32[512]{0:T(512)} %param.16) | copy-start | bytes 6148
  30.0 103.4 %copy-start.45 = (pred[1536]{0:T(1024)(128)(4,1)}, pred[1536]{0:T(1024)(128)(4,1)S(1)}, u32[]{:S(2)}) copy-start(pred[1536]{0:T(1024)(128)(4,1)S(1)} %compare_and_fusion) | copy-start | bytes 4612
  30.1 35.7 %copy-start.47 = (bf16[512,1024]{1,0:T(8,128)(2,1)S(1)}, bf16[512,1024]{1,0:T(8,128)(2,1)}, u32[]{:S(2)}) copy-start(bf16[512,1024]{1,0:T(8,128)(2,1)} %param.17) | copy-start | bytes 3145732
  67.6 2.7 copy-start.3
  67.6 2.7 copy-start.10
  67.6 2.6 copy-start.11
  67.6 2.6 copy-start.12
  67.7 2.6 copy-start.13
  67.7 2.6 copy-start.14
  67.7 2.6 copy-start.15
  67.7 2.6 copy-start.16
  67.7 2.6 copy-start.17
  67.7 2.6 copy-start.18
  67.7 2.6 copy-start.19
  67.7 2.6 copy-start.20
  67.8 2.6 copy-start.21
  67.8 2.6 copy-start.22
  67.8 2.6 copy-start.23
  67.8 2.6 copy-start.24
  67.8 2.6 copy-start.25
  67.8 2.6 copy-start.26
  67.8 2.6 copy-start.27
  67.8 2.6 copy-start.28
  67.9 2.6 copy-start.29
  67.9 2.6 copy-start.30
  67.9 2.6 copy-start.31
  67.9 2.6 copy-start.32
  67.9 2.6 copy-start.33
  67.9 2.6 copy-start.34
  70.3 58.9 %copy-start.40 = (f32[512]{0:T(512)S(1)}, f32[512]{0:T(512)}, u32[]{:S(2)}) copy-start(f32[512]{0:T(512)} %param.19) | copy-start | bytes 6148
  70.3 58.9 %copy-start.42 = (f32[512]{0:T(512)S(1)}, f32[512]{0:T(512)}, u32[]{:S(2)}) copy-start(f32[512]{0:T(512)} %param.20) | copy-start | bytes 6148
  129.2 4.2 copy-start.5
  129.2 4.2 copy-start.48
  133.4 4.3 copy-start.4
  179.0 6.1 %copy-start.44 = (f32[512]{0:T(512)}, f32[512]{0:T(512)S(1)}, u32[]{:S(2)}) copy-start(f32[512]{0:T(512)S(1)} %get-tuple-element.72) | copy-start | bytes 6148
  185.2 15.7 %copy-start.2 = (f32[1536,512]{1,0:T(8,128)}, f32[1536,512]{1,0:T(8,128)S(1)}, u32[]{:S(2)}) copy-start(f32[1536,512]{1,0:T(8,128)S(1)} %get-tuple-element.80) | copy-start | bytes 9437188
  208.4 145.4 %reduce-scatter.8.cloned.1.call-start = ((), (), s32[]{:S(2)}) async-start(), calls=%async_computation.6 | async-start | bytes 1179648 | tf_op jit(solution)/shard_map/reduce_scatter | solution.py:164
  212.5 212.5 %reduce-scatter.6.cloned.1.call-start = ((), (), s32[]{:S(2)}) async-start(), calls=%async_computation.5 | async-start | bytes 2359296 | tf_op jit(solution)/shard_map/reduce_scatter | solution.py:163
  261.9 5.9 %copy-start.7 = (bf16[1536,512]{1,0:T(8,128)(2,1)S(1)}, bf16[1536,512]{1,0:T(8,128)(2,1)}, u32[]{:S(2)}) copy-start(bf16[1536,512]{1,0:T(8,128)(2,1)} %copy-done.6) | copy-start | bytes 4718596
  279.2 5.2 %copy-start.49 = (u32[32]{0:T(128)S(1)}, u32[32]{0:T(128)}, u32[]{:S(2)}) copy-start(u32[32]{0:T(128)} %constant.240) | copy-start | bytes 388
  279.2 76.2 %all-to-all-start.1 = ((bf16[8,4,48,512]{3,2,1,0:T(8,128)(2,1)}), bf16[8,4,48,512]{3,2,1,0:T(8,128)(2,1)}, u32[]{:S(2)}, u32[]{:S(2)}) async-start(bf16[8,4,48,512]{3,2,1,0:T(8,128)(2,1)} %bitcast.73), calls=%async_computation.1 | async-start | bytes 3145728 | tf_op jit(solution)/shard_map/all_to_all | solution.py:152
  284.4 174.7 %all-reduce.9.cloned.1.call-start = ((), (), s32[]{:S(2)}) async-start(), calls=%async_computation.8 | async-start | bytes 393216 | tf_op jit(solution)/shard_map/psum | solution.py:169
  (8 other events, 16.4 us)
Sparse Core Ops, SparseCore 0:
  208.5 61.9 reduce-scatter.9
  273.9 79.8 reduce-scatter.7
  357.4 67.6 reduce-scatter.5
  427.9 31.1 all-reduce.8
where the time goes:
time: 470 us; the launch traced here: 469 us
  other arithmetic  155 us (33%)
  waiting for transfers between devices  136 us (29%)
  blocking collectives  107 us (23%)
  local copies, waits for them, and re-layouts  21.6 us (5%)
  matrix products  20.6 us (4%)
  between operations  15.4 us (3%)
  starting transfers between devices  12.8 us (3%)
    reduce_scatter x1, waiting for transfers between devices, local(): lax.psum_scatter(grad_win, 'bucket', scatter_dimension=0, tiled=True)  67.6 us
    add x1, other arithmetic, conv_backward(): grad_gated + jnp.where(same_back, grad_pad[:, back_start:back_start + len...  49.1 us
    psum x1, blocking collectives, local(): lax.psum((jnp.sum(grad_bn_rows, axis=0), jnp.sum(grad_bn_rows * bn_normed...  41.4 us
    psum x1, blocking collectives, local(): lax.psum((jnp.sum(masked, axis=0), jnp.sum(masked * masked, axis=0)), ('d...  37.9 us
    psum x1, waiting for transfers between devices, local(): lax.psum(row_sums[0].astype(jnp.bfloat16), 'dp').astype(jnp.float32)  31.1 us
    all_to_all x1, waiting for transfers between devices, local(): lax.all_to_all(outgoing, 'bucket', split_axis=0, concat_axis=0, tiled=True)  29.7 us
    reduce_sum x5, other arithmetic, conv_backward(): grad_cols.append(jnp.sum(shifted * grad_conv, axis=(0, 1)))  27.7 us
    unnamed x1, blocking collectives  21.9 us
  transfers between devices with their start and end apart: 6, of which 4 were waited for; matrix products, arithmetic and copies ran while one was open for 24% of the time, Pallas kernels for 0%

commit v1 on v0

--- a/solution.py
+++ b/solution.py
@@ -4,6 +4,12 @@
 from jax.sharding import PartitionSpec as P
 
 EPSILON = 1e-05
+
+
+def summed_here(shard, axis):
+    shards = lax.all_gather(shard, axis, axis=0, tiled=False)
+    total = shards.sum(axis=0)
+    return total
 
 
 def normalize_rows(frame_rows, ln_gain):
@@ -166,7 +172,7 @@
         lax.psum_scatter(grad_ln, "bucket", scatter_dimension=0, tiled=True),
     )
     shares = (
-        lax.psum(row_sums[0].astype(jnp.bfloat16), "dp").astype(jnp.float32),
+        summed_here(row_sums[0].astype(jnp.bfloat16), "dp").astype(jnp.float32),
         lax.psum(row_sums[1].astype(jnp.bfloat16), "dp").astype(jnp.float32),
         lax.psum(row_sums[2].astype(jnp.bfloat16), "dp").astype(jnp.float32),
         lax.psum(row_sums[3].astype(jnp.bfloat16), "dp").astype(jnp.float32),

time: 470 us -> 401 us (0.85)
  waiting for transfers between devices: 136 us -> 57.9 us
  blocking collectives: 107 us -> 115 us
    reduce_scatter x1, waiting for transfers between devices: 67.6 us -> 28.1 us  [local(): lax.psum_scatter(grad_win, 'bucket', scatter_dimension=0, tiled=True)]
    psum x1, waiting for transfers between devices: 31.1 us -> 0.01 us  [local(): lax.psum(row_sums[1].astype(jnp.bfloat16), 'dp').astype(jnp.float32)]
    reduce_scatter x1, waiting for transfers between devices: 7.68 us -> 0.01 us  [local(): lax.psum_scatter(grad_wout, 'bucket', scatter_dimension=0, tiled=True)]
    all_gather x0 -> x1, blocking collectives: none -> 7.14 us  [summed_here(): shards = lax.all_gather(shard, axis, axis=0, tiled=False)]
  transfers between devices with their start and end apart: 6 -> 6, of which waited for: 4 -> 2; matrix products, arithmetic and copies ran while one was open for 24% -> 37% of each run, Pallas kernels for 0% -> 0%
where the time goes in v1:
time: 401 us; the launch traced here: 400 us
  other arithmetic  153 us (38%)
  blocking collectives  115 us (29%)
  waiting for transfers between devices  57.9 us (14%)
  matrix products  23.5 us (6%)
  local copies, waits for them, and re-layouts  22.7 us (6%)
  between operations  15.3 us (4%)
  starting transfers between devices  12.6 us (3%)
    add x1, other arithmetic, conv_backward(): grad_gated + jnp.where(same_back, grad_pad[:, back_start:back_start + len...  47 us
    psum x1, blocking collectives, local(): lax.psum((jnp.sum(grad_bn_rows, axis=0), jnp.sum(grad_bn_rows * bn_normed...  41.7 us
    psum x1, blocking collectives, local(): lax.psum((jnp.sum(masked, axis=0), jnp.sum(masked * masked, axis=0)), ('d...  37.9 us
    all_to_all x1, waiting for transfers between devices, local(): lax.all_to_all(outgoing, 'bucket', split_axis=0, concat_axis=0, tiled=True)  29.7 us
    reduce_scatter x1, waiting for transfers between devices, local(): lax.psum_scatter(grad_win, 'bucket', scatter_dimension=0, tiled=True)  28.1 us
    reduce_sum x5, other arithmetic, conv_backward(): grad_cols.append(jnp.sum(shifted * grad_conv, axis=(0, 1)))  27.7 us
    unnamed x1, blocking collectives  21.8 us
    reduce_sum x1, other arithmetic, local(): jnp.sum(masked, axis=0)  20.7 us
  transfers between devices with their start and end apart: 6, of which 2 were waited for; matrix products, arithmetic and copies ran while one was open for 37% of the time, Pallas kernels for 0%

profile of v1, /device:TPU:0, one launch (start us, length us, event | category | flops | bytes accessed | tf_op | source)
XLA Modules:
  0.0 399.7 jit_solution(7504325124869062944)
XLA Ops:
  7.7 1.3 reduce.69
  9.2 0.7 fusion.118
  10.8 1.8 gather_fusion.2
  12.6 2.8 broadcast_select_fusion.1
  15.4 7.3 %all-to-all-start = ((bf16[8,4,48,512]{3,2,1,0:T(8,128)(2,1)}), bf16[8,4,48,512]{3,2,1,0:T(8,128)(2,1)}, u32[]{:S(2)}, u32[]{:S(2)}) async-start(bf16[8,4,48,512]{3,2,1,0:T(8,128)(2,1)} %bitcast.244), calls=%async_computation | async-start | bytes 3145728 | tf_op jit(solution)/shard_map/all_to_all | solution.py:90
  24.5 5.4 %gather_fusion.1 = bf16[1536,512]{1,0:T(8,128)(2,1)} fusion(bf16[768,512]{1,0:T(8,128)(2,1)S(1)} %copy-done.1, s32[2048]{0:T(1024)S(1)} %pad_clamp_fusion), kind=kCustom, calls=%fused_computation.3 | custom fusion | bytes 3151872 | tf_op jit(solution)/shard_map/jit(_take)/gather | solution.py:109
  30.0 29.7 %all-to-all-done = bf16[8,4,48,512]{3,2,1,0:T(8,128)(2,1)} async-done(((bf16[8,4,48,512]{3,2,1,0:T(8,128)(2,1)}), bf16[8,4,48,512]{3,2,1,0:T(8,128)(2,1)}, u32[]{:S(2)}, u32[]{:S(2)}) %all-to-all-start) | async-done | bytes 1572896 | tf_op jit(solution)/shard_map/all_to_all | solution.py:90
  59.8 1.7 convert_reduce_fusion
  61.6 2.1 multiply_reduce_fusion.35
  63.8 2.0 multiply_convert_fusion.3
  65.8 1.1 copy-done.6
  66.9 3.0 fusion.119
  70.3 1.4 select_convert_fusion.1
  71.7 0.9 copy-done.3
  72.9 20.7 %select_reduce_fusion = (f32[512]{0:T(512)S(1)}, f32[512]{0:T(512)S(1)}, f32[32,48,512]{2,1,0:T(8,128)}) fusion(pred[32,48]{1,0:T(8,128)(4,1)S(1)} %iota_compare_fusion.3, f32[512]{0:T(512)S(1)} %bitcast.357, pred[32,48]{1,0:T(8,128)(4,1)S(1)} %bitcast.325, f32[512]{0:T(512)S(1)} %bitcast.359, pred[32,48]{1,0:T(8,128)(4,1)S(1)} %bitcast.322, ...), kind=kLoop, calls=%fused_computation.243 | loop fusion | flops 99089408 | bytes 4833792 | tf_op jit(solution)/shard_map/reduce_sum | solution.py:121
  93.6 37.9 %all-reduce.4 = (f32[512]{0:T(512)S(1)}, f32[512]{0:T(512)S(1)}) all-reduce(f32[512]{0:T(512)S(1)} %get-tuple-element.42, f32[512]{0:T(512)S(1)} %get-tuple-element.41), channel_id=1, replica_groups=mesh['dp'=4,'bucket'=8] {'dp','bucket'}, use_global_device_ids=true, to_apply=%region_11.13 | all-reduce | flops 1024 | bytes 8192 | tf_op jit(solution)/shard_map/psum | solution.py:120
  131.5 4.7 %multiply_convert_fusion.2 = (bf16[1536,512]{1,0:T(8,128)(2,1)S(1)}, f32[1536,512]{1,0:T(8,128)}) fusion(f32[512]{0:T(512)S(1)} %copy-done.41, f32[512]{0:T(512)S(1)} %copy-done.39, f32[512]{0:T(512)S(1)} %get-tuple-element.82, f32[512]{0:T(512)S(1)} %get-tuple-element.125, f32[32,48,512]{2,1,0:T(8,128)} %get-tuple-element.89), kind=kLoop, calls=%fused_computation.204 | loop fusion | flops 7077888 | bytes 7872512 | tf_op jit(solution)/shard_map/convert_element_type | solution.py:129
  136.2 1.1 copy-done.5
  137.3 2.2 fusion.110
  139.5 5.5 %fusion.111 = (f32[512]{0:T(512)S(1)}, f32[512]{0:T(512)S(1)}, f32[1536,512]{1,0:T(8,128)}) fusion(f32[1536,512]{1,0:T(8,128)} %get-tuple-element.88, f32[512]{0:T(512)S(1)} %copy-done.41, f32[512]{0:T(512)S(1)} %copy-done.39, bf16[512,512]{1,0:T(8,128)(2,1)} %param.21, bf16[1536,512]{1,0:T(8,128)(2,1)} %gather_fusion.1, ...), kind=kOutput, calls=%fused_computation.339 | convolution fusion | flops 817101824 | bytes 8399872 | tf_op jit(solution)/shard_map/re,de->rd/dot_general | solution.py:133
  145.0 41.7 %all-reduce.3 = (f32[512]{0:T(512)S(1)}, f32[512]{0:T(512)S(1)}) all-reduce(f32[512]{0:T(512)S(1)} %get-tuple-element.45, f32[512]{0:T(512)S(1)} %get-tuple-element.44), channel_id=1, replica_groups=mesh['dp'=4,'bucket'=8] {'dp','bucket'}, use_global_device_ids=true, to_apply=%region_15.17 | all-reduce | flops 1024 | bytes 8192 | tf_op jit(solution)/shard_map/psum | solution.py:135
  187.3 5.5 %multiply_reduce_fusion.16 = (f32[512]{0:T(512)S(1)}, f32[1536,512]{1,0:T(8,128)S(1)}) fusion(f32[1536,512]{1,0:T(8,128)} %get-tuple-element.88, f32[512]{0:T(512)S(1)} %get-tuple-element.162, f32[1536,512]{1,0:T(8,128)} %get-tuple-element.160, f32[512]{0:T(512)S(1)} %get-tuple-element.163, f32[512]{0:T(512)S(1)} %get-tuple-element.81, ...), kind=kLoop, calls=%fused_computation.182 | loop fusion | flops 11009536 | bytes 15738368 | tf_op jit(solution)/shard_map/reduce_sum | solution.py:55
  192.9 7.1 %multiply_reduce_fusion.10 = (f32[512]{0:T(512)S(1)}, f32[512]{0:T(512)S(1)}, f32[512]{0:T(512)S(1)}, f32[512]{0:T(512)S(1)}, f32[512]{0:T(512)S(1)}, /*index=5*...) fusion(f32[32,48,512]{2,1,0:T(8,128)S(1)} %bitcast.234, pred[32,48]{1,0:T(8,128)(4,1)S(1)} %bitcast.299, ...), kind=kLoop, calls=%fused_computation.176 | loop fusion | flops 28306944 | bytes 4750848 | tf_op jit(solution)/shard_map/reduce_sum | solution.py:55
  200.0 6.7 %multiply_reduce_fusion.20 = (f32[512]{0:T(512)S(1)}, f32[512]{0:T(512)S(1)}, f32[512]{0:T(512)S(1)}, f32[512]{0:T(512)S(1)}, f32[512]{0:T(512)S(1)}, /*index=5*...) fusion(f32[32,48,512]{2,1,0:T(8,128)S(1)} %bitcast.235, pred[32,48]{1,0:T(8,128)(4,1)S(1)} %bitcast.272, ...), kind=kLoop, calls=%fused_computation.186 | loop fusion | flops 28306944 | bytes 4750848 | tf_op jit(solution)/shard_map/reduce_sum | solution.py:55
  206.7 1.9 multiply_reduce_fusion.29
  208.6 6.5 %multiply_reduce_fusion.1 = (f32[512]{0:T(512)S(1)}, f32[512]{0:T(512)S(1)}, f32[512]{0:T(512)S(1)}, f32[512]{0:T(512)S(1)}, f32[512]{0:T(512)S(1)}, /*index=5*/...) fusion(f32[32,48,512]{2,1,0:T(8,128)S(1)} %bitcast.237, pred[32,48]{1,0:T(8,128)(4,1)S(1)} %bitcast.326, ...), kind=kLoop, calls=%fused_computation.167 | loop fusion | flops 28306944 | bytes 4750848 | tf_op jit(solution)/shard_map/reduce_sum | solution.py:55
  215.3 0.8 copy.41
  216.2 47.0 %fusion.73 = f32[32,48,512]{2,1,0:T(8,128)} fusion(f32[32,48,512]{2,1,0:T(8,128)} %bitcast.238, f32[512]{0:T(512)S(1)} %bitcast.358, f32[512]{0:T(512)S(1)} %bitcast.360, f32[512]{0:T(512)S(1)} %bitcast.364, f32[512]{0:T(512)S(1)} %bitcast.366, f32[512]{0:T(512)S(1)} %bitcast.368, f32[512]{0:T(512)S(1)} %bitcast.370, f32[512]{0:T(512)S(1)} %bitcast.372, ...), kind=kLoop, calls=%fused_computation.139 | loop fusion | flops 71565312 | bytes 6401024 | tf_op jit(solution)/shard_map/add | solution.py:59
  263.3 5.8 %multiply_convert_fusion.1 = (bf16[1536,512]{1,0:T(8,128)(2,1)}, bf16[1536,512]{1,0:T(8,128)(2,1)}) fusion(f32[32,48,512]{2,1,0:T(8,128)} %fusion.73, pred[1536]{0:T(1024)(128)(4,1)S(1)} %lt.126, f32[1536,1024]{1,0:T(8,128)} %copy-done.3), kind=kLoop, calls=%fused_computation.201 | loop fusion | flops 8650752 | bytes 12584448 | tf_op jit(solution)/shard_map/convert.2
  269.1 1.5 convert_element_type.235
  270.9 5.1 %fusion.95 = f32[512,1024]{1,0:T(8,128)} fusion(bf16[1536,512]{1,0:T(8,128)(2,1)S(1)} %copy-done.7, bf16[1536,512]{1,0:T(8,128)(2,1)} %get-tuple-element.91, bf16[1536,512]{1,0:T(8,128)(2,1)} %get-tuple-element.90), kind=kOutput, calls=%fused_computation.246 | convolution fusion | flops 1616904192 | bytes 6815744 | tf_op jit(solution)/shard_map/rd,rf->df/dot_general | solution.py:152
  276.0 5.3 %multiply_reduce_fusion = (f32[512]{0:T(512)S(1)}, f32[1536]{0:T(1024)S(1)}, f32[1536]{0:T(1024)S(1)}, f32[1536,512]{1,0:T(8,128)S(1)}) fusion(bf16[8,4,48,512]{3,2,1,0:T(8,128)(2,1)} %all-to-all-done, f32[1536]{0:T(1024)S(1)} %rsqrt.15, f32[1536]{0:T(1024)S(1)} %div.33, f32[512]{0:T(512)S(1)} %copy-done.40, bf16[512,1024]{1,0:T(8,128)(2,1)} %param.17, ...), kind=kOutput, calls=%fused_computation.166 | convolution fusion | flops 1623978496 | bytes 8941568 | tf_op jit(solution)/shard_map/rf,df->rd/dot_general | solution.py:153
  281.4 3.4 select_convert_fusion
  284.8 5.0 %all-to-all-start.1 = ((bf16[8,4,48,512]{3,2,1,0:T(8,128)(2,1)}), bf16[8,4,48,512]{3,2,1,0:T(8,128)(2,1)}, u32[]{:S(2)}, u32[]{:S(2)}) async-start(bf16[8,4,48,512]{3,2,1,0:T(8,128)(2,1)} %bitcast.73), calls=%async_computation.1 | async-start | bytes 3145728 | tf_op jit(solution)/shard_map/all_to_all | solution.py:158
  291.8 4.5 %fusion.102 = (s32[768]{0:T(1024)S(1)}, s32[768,1]{0,1:T(1,128)S(1)}) fusion(s32[]{:T(128)} %bitcast.25, s32[]{:T(128)} %bitcast.26, s32[]{:T(128)} %bitcast.27, s32[]{:T(128)} %bitcast.28, s32[]{:T(128)} %bitcast.29, s32[]{:T(128)} %bitcast.31, s32[]{:T(128)} %bitcast.30, s32[768]{0:T(1024)S(1)} %get-tuple-element.124, s32[768]{0:T(1024)S(1)} %get-tuple-element.123), kind=kLoop, calls=%fused_computation.316 | loop fusion | flops 10752 | bytes 12316 | tf_op jit(solution)/shard_map/jit(_take)/gather | solution.py:100
  297.2 15.7 %compare_and_fusion.1 = (pred[768]{0:T(1024)(128)(4,1)S(1)}, s32[768]{0:T(1024)S(1)}) fusion(s32[768]{0:T(1024)S(1)} %convert_reduce_fusion.1, pred[768]{0:T(1024)(128)(4,1)S(1)} %get-tuple-element.70, pred[768]{0:T(1024)(128)(4,1)S(1)} %get-tuple-element.68, pred[768]{0:T(1024)(128)(4,1)S(1)} %get-tuple-element.69, ...), kind=kLoop, calls=%fused_computation.315 | loop fusion | flops 32256 | bytes 29284 | tf_op jit(solution)/shard_map/jit(_take)/and | solution.py:131
  313.0 2.5 convolution_convert_fusion
  315.5 3.3 gather_fusion
  318.8 21.8 %all-reduce.2 = bf16[512]{0:T(512)(128)(2,1)S(1)} all-reduce(f32[512]{0:T(512)S(1)} %get-tuple-element.9), channel_id=6, replica_groups=mesh['dp'=4,'bucket'=8] {'bucket'}, use_global_device_ids=true, to_apply=%region_56.58.clone | all-reduce | flops 512 | bytes 3072
  340.7 2.2 broadcast_select_fusion.2
  342.9 0.8 copy.42
  343.7 6.3 %all-reduce.5 = (bf16[64,31]{0,1:T(8,128)(2,1)S(1)}, bf16[64]{0:T(256)(128)(2,1)S(1)}) all-reduce(bf16[64,31]{0,1:T(8,128)(2,1)S(1)} %copy.42, bf16[64]{0:T(256)(128)(2,1)S(1)} %dynamic-slice.3), channel_id=1, replica_groups=mesh['dp'=4,'bucket'=8] {'dp'}, use_global_device_ids=true, to_apply=%region_54.56 | all-reduce | flops 2048 | bytes 8192 | tf_op jit(solution)/shard_map/psum | solution.py:177
  351.2 1.5 convert_element_type.236
  352.7 2.1 gather_fusion.3
  354.7 1.4 broadcast_select_fusion
  356.1 28.1 %reduce-scatter.6.cloned.1.call-done = f32[64,1024]{1,0:T(8,128)} async-done(((f32[512,1024]{1,0:T(8,128)}), f32[64,1024]{1,0:T(8,128)}) %reduce-scatter.6.cloned.1.call-update) | async-done | bytes 262160 | tf_op jit(solution)/shard_map/reduce_scatter | solution.py:169
  384.2 1.0 convert_element_type.233
  385.2 7.1 %all-gather = bf16[256,1024]{1,0:T(8,128)(2,1)S(1)} all-gather(bf16[64,1024]{1,0:T(8,128)(2,1)S(1)} %convert_element_type.233), channel_id=2, replica_groups=mesh['dp'=4,'bucket'=8] {'dp'}, dimensions={0}, use_global_device_ids=true | all-gather | bytes 655360 | tf_op jit(solution)/shard_map/all_gather | solution.py:10
  (156 shorter events, 9.2 us)
Async XLA Ops:
  7.2 3.6 copy-start
  12.6 10.2 %copy-start.44 = (s32[1,256]{1,0:T(1,128)S(1)}, s32[1,256]{1,0:T(1,128)}, u32[]{:S(2)}) copy-start(s32[1,256]{1,0:T(1,128)} %param.13) | copy-start | bytes 3076
  12.6 12.0 %copy-start.1 = (bf16[768,512]{1,0:T(8,128)(2,1)S(1)}, bf16[768,512]{1,0:T(8,128)(2,1)}, u32[]{:S(2)}) copy-start(bf16[768,512]{1,0:T(8,128)(2,1)} %param.15) | copy-start | bytes 2359300
  15.4 44.4 %all-to-all-start = ((bf16[8,4,48,512]{3,2,1,0:T(8,128)(2,1)}), bf16[8,4,48,512]{3,2,1,0:T(8,128)(2,1)}, u32[]{:S(2)}, u32[]{:S(2)}) async-start(bf16[8,4,48,512]{3,2,1,0:T(8,128)(2,1)} %bitcast.244), calls=%async_computation | async-start | bytes 3145728 | tf_op jit(solution)/shard_map/all_to_all | solution.py:90
  22.7 246.4 %reduce-scatter.8.cloned.1.call-start = ((), (), s32[]{:S(2)}) async-start(), calls=%async_computation.6 | async-start | bytes 1179648 | tf_op jit(solution)/shard_map/reduce_scatter | solution.py:170
  24.5 5.4 %copy-start.8 = (f32[512,31]{0,1:T(8,128)S(1)}, f32[512,31]{0,1:T(8,128)}, u32[]{:S(2)}) copy-start(f32[512,31]{0,1:T(8,128)} %param.18) | copy-start | bytes 190468
  29.9 33.8 %copy-start.40 = (f32[512]{0:T(512)S(1)}, f32[512]{0:T(512)}, u32[]{:S(2)}) copy-start(f32[512]{0:T(512)} %param.16) | copy-start | bytes 6148
  69.9 2.7 copy-start.3
  70.0 2.7 copy-start.9
  70.0 2.6 copy-start.10
  70.0 2.6 copy-start.11
  70.0 2.6 copy-start.12
  70.0 2.6 copy-start.13
  70.0 2.6 copy-start.14
  70.0 2.6 copy-start.15
  70.0 2.6 copy-start.16
  70.1 2.6 copy-start.17
  70.1 2.6 copy-start.18
  70.1 2.6 copy-start.19
  70.1 2.6 copy-start.20
  70.1 2.6 copy-start.21
  70.1 2.6 copy-start.22
  70.1 2.6 copy-start.23
  70.1 2.6 copy-start.24
  70.2 2.6 copy-start.25
  70.2 2.6 copy-start.26
  70.2 2.6 copy-start.27
  70.2 2.6 copy-start.28
  70.2 2.6 copy-start.29
  70.2 2.6 copy-start.30
  70.2 2.6 copy-start.31
  70.2 2.6 copy-start.32
  70.3 2.6 copy-start.33
  70.3 2.6 copy-start.34
  70.3 2.6 copy-start.35
  70.3 2.6 copy-start.36
  70.3 2.6 copy-start.37
  72.6 58.8 %copy-start.39 = (f32[512]{0:T(512)S(1)}, f32[512]{0:T(512)}, u32[]{:S(2)}) copy-start(f32[512]{0:T(512)} %param.19) | copy-start | bytes 6148
  72.6 58.9 %copy-start.41 = (f32[512]{0:T(512)S(1)}, f32[512]{0:T(512)}, u32[]{:S(2)}) copy-start(f32[512]{0:T(512)} %param.20) | copy-start | bytes 6148
  131.5 5.8 %copy-start.4 = (bf16[1536,512]{1,0:T(8,128)(2,1)S(1)}, bf16[1536,512]{1,0:T(8,128)(2,1)}, u32[]{:S(2)}) copy-start(bf16[1536,512]{1,0:T(8,128)(2,1)} %gather_fusion.1) | copy-start | bytes 4718596
  139.5 203.4 %reduce-scatter.10.cloned.1.call-start = ((), (), s32[]{:S(2)}) async-start(), calls=%async_computation.8 | async-start | bytes 294912
  186.8 6.1 %copy-start.43 = (f32[512]{0:T(512)}, f32[512]{0:T(512)S(1)}, u32[]{:S(2)}) copy-start(f32[512]{0:T(512)S(1)} %get-tuple-element.72) | copy-start | bytes 6148
  192.9 15.7 %copy-start.2 = (f32[1536,512]{1,0:T(8,128)}, f32[1536,512]{1,0:T(8,128)S(1)}, u32[]{:S(2)}) copy-start(f32[1536,512]{1,0:T(8,128)S(1)} %get-tuple-element.78) | copy-start | bytes 9437188
  216.2 135.0 %all-reduce.8.cloned.1.call-start = ((), (), s32[]{:S(2)}) async-start(), calls=%async_computation.7 | async-start | bytes 131072 | tf_op jit(solution)/shard_map/psum | solution.py:176
  263.2 7.7 %copy-start.7 = (bf16[1536,512]{1,0:T(8,128)(2,1)S(1)}, bf16[1536,512]{1,0:T(8,128)(2,1)}, u32[]{:S(2)}) copy-start(bf16[1536,512]{1,0:T(8,128)(2,1)} %copy-done.6) | copy-start | bytes 4718596
  270.7 113.6 %reduce-scatter.6.cloned.1.call-start = ((), (), s32[]{:S(2)}) async-start(), calls=%async_computation.5 | async-start | bytes 2359296 | tf_op jit(solution)/shard_map/reduce_scatter | solution.py:169
  284.8 5.0 %copy-start.45 = (u32[32]{0:T(128)S(1)}, u32[32]{0:T(128)}, u32[]{:S(2)}) copy-start(u32[32]{0:T(128)} %constant.241) | copy-start | bytes 388
  284.8 67.9 %all-to-all-start.1 = ((bf16[8,4,48,512]{3,2,1,0:T(8,128)(2,1)}), bf16[8,4,48,512]{3,2,1,0:T(8,128)(2,1)}, u32[]{:S(2)}, u32[]{:S(2)}) async-start(bf16[8,4,48,512]{3,2,1,0:T(8,128)(2,1)} %bitcast.73), calls=%async_computation.1 | async-start | bytes 3145728 | tf_op jit(solution)/shard_map/all_to_all | solution.py:158
  (4 other events, 5.4 us)
Sparse Core Ops, SparseCore 0:
  139.6 65.3 reduce-scatter.7
  216.3 61.8 reduce-scatter.9
  281.0 30.5 all-reduce.7
  315.1 69.1 reduce-scatter.5
